TPU v7x, 256 devices: a whole 4x4x8 slice. The times are simulated.
256 devices in a mesh: phase: 16 (over y_hi, x, core), chan: 16 (over z, y_lo).
Axes of the slice: x: 4, y: 4 (y_hi: 2, y_lo: 2; y = y_hi * 2 + y_lo), z: 8, core: 2. Of those that a mesh axis runs over, the one named last changes fastest.
Arguments:
- frames: bfloat16 [64, 32, 2048], P(None, 'phase', 'chan'), may hold values from -6 to 6
- temporal_taps: float32 [4, 3, 64], replicated, may hold values from -3 to 3
- conv_weights: bfloat16 [4, 64, 27, 2, 64], P(None, None, None, None, 'chan'), may hold values from -0.15625 to 0.15625
- cotangent: bfloat16 [64, 32, 2048], P(None, 'phase', 'chan'), may hold values from -16 to 16
Outputs:
- final_frames: bfloat16 [64, 32, 2048], P(None, 'phase', 'chan')
- grad_frames: bfloat16 [64, 32, 2048], P(None, 'phase', 'chan')
- grad_taps: float32 [4, 3, 64], replicated
- grad_weights: float32 [4, 64, 27, 2, 64], P(None, None, None, None, 'chan')
All inputs are finite; a program needn't handle non-finite values.
Results may differ from a plain program's by a relative error of at most 0.025.
Values may be sent and summed in bfloat16 or wider, within the bound.
No kernel may reach another device: no remote copies, remote signals or barrier semaphores. Data moves between devices by JAX's collectives and lax.ppermute only.
A program may use at most 64 MiB of HBM per device.

v0:
```python
import jax
import jax.numpy as jnp
from jax import lax
from jax.sharding import PartitionSpec as P

BLOCKS = 4
SY = 8
SZ = 16
cell_offsets = [
    (kernel_pos // 9 - 1, kernel_pos // 3 % 3 - 1, kernel_pos % 3 - 1) for kernel_pos in range(27)
]


def shifted(block, axis, distance):
    devices = range(lax.axis_size(axis))
    route = [((i - distance) % len(devices), i) for i in devices]
    return lax.ppermute(block, axis, route)


def padded_2(cells, sides, width):
    for axis, dim in sides:
        count = lax.axis_size(axis)
        ends = count - 1
        head = lax.slice_in_dim(cells, 0, width, axis=dim)
        tail = lax.slice_in_dim(cells, cells.shape[dim] - width, cells.shape[dim], axis=dim)
        cells = jnp.concatenate(
            [
                lax.ppermute(tail, axis, [(i, (i + 1) % count) for i in range(ends)]),
                cells,
                lax.ppermute(head, axis, [((i + 1) % count, i) for i in range(ends)]),
            ],
            axis=dim,
        )
    return cells


def within_plane(source, step_y, step_z):
    cell_count = source.shape[-1]
    last_dim = source.ndim - 1
    margin = SZ + 1
    moved = step_y * SZ + step_z
    padded = jnp.pad(source, [(0, 0)] * last_dim + [(margin, margin)])
    window = lax.slice_in_dim(padded, margin + moved, margin + moved + cell_count, axis=last_dim)
    places = jnp.arange(cell_count, dtype=jnp.int32)
    coord_y = places // SZ + step_y
    coord_z = places % SZ + step_z
    inside = (coord_y >= 0) & (coord_y < SY) & (coord_z >= 0) & (coord_z < SZ)
    return jnp.where(inside, window, jnp.zeros_like(window))


def shifted_cells(rimmed, step_x, step_y, step_z):
    planes = rimmed.shape[-2] - 2
    rows = lax.slice_in_dim(rimmed, 1 + step_x, 1 + step_x + planes, axis=rimmed.ndim - 2)
    moved = within_plane(rows, step_y, step_z)
    return moved.reshape(moved.shape[:-2] + (planes * moved.shape[-1],))


def offset_stack(rimmed, first, count, sign):
    picked = cell_offsets[first : first + count]
    return jnp.stack(
        [
            shifted_cells(rimmed, sign * offset[0], sign * offset[1], sign * offset[2])
            for offset in picked
        ],
        axis=1,
    )


def back_block(source, hops):
    if hops == 0:
        return source
    return shifted(source, "phase", hops)


def next_block(source, hops):
    if hops == 0:
        return source
    return shifted(source, "phase", -hops)


def neighbours(source, reach):
    phase_rows = source.shape[1]
    hops, rest = divmod(reach, phase_rows)
    if rest == 0:
        return (back_block(source, hops), next_block(source, hops))
    joined = jnp.concatenate([back_block(source, hops + 1), back_block(source, hops)], axis=1)
    behind = joined[:, phase_rows - rest : 2 * phase_rows - rest]
    joined = jnp.concatenate([next_block(source, hops), next_block(source, hops + 1)], axis=1)
    ahead = joined[:, rest : rest + phase_rows]
    return (behind, ahead)


def per_device(frames, temporal_taps, conv_weights, cotangent):
    chans, phase_rows, cell_count = frames.shape
    plane_cells = SY * SZ
    planes = cell_count // plane_cells
    state = frames
    saved = []
    for block_num in range(BLOCKS):
        reach = 2**block_num
        behind, ahead = neighbours(state, reach)
        tap_rows = temporal_taps[block_num][:, :, None, None]
        mixed = (
            tap_rows[0] * behind.astype(jnp.float32)
            + tap_rows[1] * state.astype(jnp.float32)
            + tap_rows[2] * ahead.astype(jnp.float32)
        ).astype(jnp.bfloat16)
        rimmed = padded_2(mixed.reshape(chans, phase_rows, planes, plane_cells), (("chan", 2),), 1)
        kernel = lax.all_gather(conv_weights[block_num], "chan", axis=3, tiled=True)
        conv_out = jnp.zeros((chans, 2, phase_rows, cell_count), jnp.float32)
        for first in range(0, 27, 9):
            group = offset_stack(rimmed, first, 9, 1)
            conv_out = conv_out + jnp.einsum(
                "ikpv,ikgo->ogpv",
                group,
                kernel[:, first : first + 9],
                preferred_element_type=jnp.float32,
            )
        value_part = conv_out[:, 0]
        gate_sig = jax.nn.sigmoid(conv_out[:, 1])
        saved.append((state, behind, ahead, rimmed, kernel, value_part, gate_sig))
        state = (state.astype(jnp.float32) + value_part * gate_sig).astype(jnp.bfloat16)
    grad_state = cotangent
    weight_grads = [None] * BLOCKS
    tap_grads = [None] * BLOCKS
    for block_num in reversed(range(BLOCKS)):
        reach = 2**block_num
        prior, behind, ahead, rimmed, kernel, value_part, gate_sig = saved[block_num]
        tap_rows = temporal_taps[block_num][:, :, None, None]
        grad_y = grad_state.astype(jnp.float32)
        grad_z = jnp.stack(
            [grad_y * gate_sig, grad_y * value_part * gate_sig * (1.0 - gate_sig)], axis=1
        ).astype(jnp.bfloat16)
        rim_grad = padded_2(
            grad_z.reshape(chans, 2, phase_rows, planes, plane_cells), (("chan", 3),), 1
        )
        grad_mix = jnp.zeros((chans, phase_rows, cell_count), jnp.float32)
        for first in range(0, 27, 3):
            group = offset_stack(rim_grad, first, 3, -1)
            grad_mix = grad_mix + jnp.einsum(
                "okgpv,ikgo->ipv",
                group,
                kernel[:, first : first + 3],
                preferred_element_type=jnp.float32,
            )
        kernel_parts = []
        for first in range(0, 27, 9):
            group = offset_stack(rimmed, first, 9, 1)
            kernel_parts.append(
                jnp.einsum("ikpv,ogpv->ikgo", group, grad_z, preferred_element_type=jnp.float32)
            )
        grad_kernel = jnp.concatenate(kernel_parts, axis=1)
        grad_tap = jnp.stack(
            [
                jnp.sum(grad_mix * behind.astype(jnp.float32), axis=(1, 2)),
                jnp.sum(grad_mix * prior.astype(jnp.float32), axis=(1, 2)),
                jnp.sum(grad_mix * ahead.astype(jnp.float32), axis=(1, 2)),
            ]
        )
        grad_low = grad_mix.astype(jnp.bfloat16)
        back_mix, ahead_mix = neighbours(grad_low, reach)
        grad_state = (
            grad_y
            + tap_rows[0] * ahead_mix.astype(jnp.float32)
            + tap_rows[1] * grad_low.astype(jnp.float32)
            + tap_rows[2] * back_mix.astype(jnp.float32)
        ).astype(jnp.bfloat16)
        kernel_piece = lax.psum_scatter(
            grad_kernel.astype(jnp.bfloat16), "chan", scatter_dimension=3, tiled=True
        )
        grad_kernel = lax.psum(kernel_piece, "phase").astype(jnp.float32)
        weight_grads[block_num] = grad_kernel
        tap_grads[block_num] = grad_tap
    grad_weights = jnp.stack(weight_grads)
    grad_taps = lax.psum(jnp.stack(tap_grads), ("phase", "chan"))
    return (state, grad_state, grad_taps, grad_weights)


def solution(mesh):
    in_specs = (
        P(None, "phase", "chan"),
        P(),
        P(None, None, None, None, "chan"),
        P(None, "phase", "chan"),
    )
    out_specs = (
        P(None, "phase", "chan"),
        P(None, "phase", "chan"),
        P(),
        P(None, None, None, None, "chan"),
    )
    return jax.shard_map(
        per_device, mesh=mesh, in_specs=in_specs, out_specs=out_specs, check_vma=False
    )
```

profile of v0, /device:TPU:7, one launch (start us, length us, event | category | flops | bytes accessed | tf_op | source)
XLA Modules:
  0.0 648.9 jit_solution(4640616665763876973)
XLA Ops:
  8.0 3.4 collective-permute-start
  12.5 34.2 %all-gather = bf16[1,64,27,2,64]{1,3,2,0,4:T(2,128)(2,1)S(1)} all-gather(bf16[1,64,27,2,4]{1,3,2,0,4:T(2,128)(2,1)S(1)} %copy.558), channel_id=2, replica_groups=mesh['phase'=16,'chan'=16] {'chan'}, dimensions={4}, use_global_device_ids=true | all-gather | bytes 470016 | tf_op jit(solution)/shard_map/all_gather | solution.py:109
  47.5 1.3 collective-permute-start.3
  49.0 4.0 collective-permute-start.2
  56.6 13.0 %collective-permute-start.4 = (bf16[64,2,128]{2,0,1:T(8,128)(2,1)S(1)}, bf16[64,2,128]{2,0,1:T(8,128)(2,1)S(1)}, u32[]{:S(2)}, u32[]{:S(2)}) collective-permute-start(bf16[64,2,128]{2,0,1:T(8,128)(2,1)S(1)} %fusion.164), channel_id=1, source_target_pairs={{240,0},{0,16},{16,32},{32,48},{48,64},{64,80},{80,96},{96,112},{1... | collective-permute-start | bytes 98312 | tf_op jit(solution)/shard_map/ppermute | solution.py:17
  70.7 5.9 collective-permute-done.5
  77.2 2.9 collective-permute-start.6
  80.1 1.3 collective-permute-start.7
  81.4 31.7 %all-gather.1 = bf16[1,64,27,2,64]{1,3,2,0,4:T(2,128)(2,1)S(1)} all-gather(bf16[1,64,27,2,4]{1,3,2,0,4:T(2,128)(2,1)S(1)} %copy.559), channel_id=3, replica_groups=mesh['phase'=16,'chan'=16] {'chan'}, dimensions={4}, use_global_device_ids=true | all-gather | bytes 470016 | tf_op jit(solution)/shard_map/all_gather | solution.py:109
  115.8 1.5 collective-permute-start.9
  117.3 1.3 collective-permute-done.8
  118.6 3.7 collective-permute-done.9
  122.9 2.8 collective-permute-start.10
  125.7 1.3 collective-permute-start.11
  127.0 33.8 %all-gather.2 = bf16[1,64,27,2,64]{1,3,2,0,4:T(2,128)(2,1)S(1)} all-gather(bf16[1,64,27,2,4]{1,3,2,0,4:T(2,128)(2,1)S(1)} %copy.560), channel_id=4, replica_groups=mesh['phase'=16,'chan'=16] {'chan'}, dimensions={4}, use_global_device_ids=true | all-gather | bytes 470016 | tf_op jit(solution)/shard_map/all_gather | solution.py:109
  163.5 3.0 collective-permute-start.13
  166.5 1.3 collective-permute-done.12
  167.7 2.5 collective-permute-done.13
  170.8 2.2 collective-permute-start.14
  173.1 1.3 collective-permute-start.15
  174.4 30.8 %all-gather.3 = bf16[1,64,27,2,64]{1,3,2,0,4:T(2,128)(2,1)S(1)} all-gather(bf16[1,64,27,2,4]{1,3,2,0,4:T(2,128)(2,1)S(1)} %copy.561), channel_id=5, replica_groups=mesh['phase'=16,'chan'=16] {'chan'}, dimensions={4}, use_global_device_ids=true | all-gather | bytes 470016 | tf_op jit(solution)/shard_map/all_gather | solution.py:109
  205.4 1.3 dynamic-slice
  212.9 1.3 collective-permute-start.16
  214.5 4.0 collective-permute-start.17
  220.1 1.1 pad_maximum_fusion.3
  225.3 2.3 collective-permute-start.18
  228.9 3.1 collective-permute-done.18
  232.1 1.4 collective-permute-start.20
  236.0 4.0 collective-permute-start.21
  240.1 1.1 pad_maximum_fusion.2
  247.8 4.1 collective-permute-done.22
  252.2 1.4 collective-permute-start.24
  253.8 4.6 collective-permute-start.25
  260.1 1.1 pad_maximum_fusion.1
  264.3 26.8 %collective-permute-start.27 = (bf16[64,2,128]{2,0,1:T(8,128)(2,1)S(1)}, bf16[64,2,128]{2,0,1:T(8,128)(2,1)S(1)}, u32[]{:S(2)}, u32[]{:S(2)}) collective-permute-start(bf16[64,2,128]{2,0,1:T(8,128)(2,1)S(1)} %get-tuple-element.46), channel_id=1, source_target_pairs={{240,0},{0,16},{16,32},{32,48},{48,64},{64,80},{80,96},{96,112},{1... | collective-permute-start | bytes 98312 | tf_op jit(solution)/shard_map/ppermute | solution.py:17
  291.1 1.0 collective-permute-done.27
  292.1 5.9 collective-permute-done.26
  298.2 1.4 collective-permute-start.28
  299.9 4.9 collective-permute-start.29
  307.1 1.2 pad_maximum_fusion
  313.8 85.8 %psum.35 = f32[4,3,64]{2,1,0:T(4,128)S(1)} all-reduce(f32[4,3,64]{2,1,0:T(4,128)S(1)} %pad_maximum_fusion.48), channel_id=1, replica_groups=mesh['phase'=16,'chan'=16] {'phase','chan'}, use_global_device_ids=true, to_apply=%region_12.13 | all-reduce | flops 768 | bytes 6144 | tf_op jit(solution)/shard_map/psum | solution.py:175
  400.2 91.4 %all-reduce.33.cloned.1.call-done = (bf16[64,27,2,64]{0,3,1,2:T(8,128)(2,1)}, bf16[64,27,2,64]{0,3,1,2:T(8,128)(2,1)}, bf16[64,27,2,64]{0,3,1,2:T(8,128)(2,1)}, bf16[64,27,2,64]{0,3,1,2:T(8,128)(2,1)}) async-done(((bf16[64,27,2,64]{0,3,1,2:T(8,128)(2,1)}, bf16[64,27,2,64]{0,3,1,2:T(8,128)(2,1)}, bf16[64,27,2,64]{0,3,1,2:T(8,128)(2,1)}, bf16[64,27,2,64]{0,3,1,2:T(8,128)(2,1)}), ...) | async-done | bytes 1769488
  491.6 1.5 dynamic-slice_bitcast_fusion
  493.1 1.5 dynamic-slice_bitcast_fusion.1
  494.7 1.6 dynamic-slice_bitcast_fusion.2
  496.2 1.5 dynamic-slice_bitcast_fusion.3
  499.2 140.9 %all-reduce.35.cloned.1.call-done = (bf16[1,64,27,2,4]{1,4,2,3,0:T(4,128)(2,1)}, bf16[1,64,27,2,4]{1,4,2,3,0:T(4,128)(2,1)}, bf16[1,64,27,2,4]{1,4,2,3,0:T(4,128)(2,1)}, bf16[1,64,27,2,4]{1,4,2,3,0:T(4,128)(2,1)}) async-done(((bf16[1,64,27,2,4]{1,4,2,3,0:T(4,128)(2,1)}, bf16[1,64,27,2,4]{1,4,2,3,0:T(4,128)(2,1)}, bf16[1,64,27,2,4]{1,4,2,3,0:T(4,128)(2,1)}, bf16[1,64,27,2,4]{1,4,2,3,0:T(4,128)(2,1)}), ...) | async-done | bytes 110608 | tf_op jit(solution)/shard_map/psum | solution.py:171
  640.1 1.1 maximum_convert_fusion
  (373 shorter events, 51.8 us)
Async XLA Ops:
  7.2 484.4 %all-reduce.33.cloned.1.call-start = ((), (), s32[]{:S(2)}) async-start(), calls=%async_computation | async-start | bytes 7077888
  8.0 38.9 %copy-start.35 = (bf16[64,2,128]{2,0,1:T(8,128)(2,1)}, bf16[64,2,128]{2,0,1:T(8,128)(2,1)S(1)}, u32[]{:S(2)}) copy-start(bf16[64,2,128]{2,0,1:T(8,128)(2,1)S(1)} %copy.143) | copy-start | bytes 98308
  8.0 38.9 %collective-permute-start = (bf16[64,2,128]{2,0,1:T(8,128)(2,1)S(1)}, bf16[64,2,128]{2,0,1:T(8,128)(2,1)S(1)}, u32[]{:S(2)}, u32[]{:S(2)}) collective-permute-start(bf16[64,2,128]{2,0,1:T(8,128)(2,1)S(1)} %copy.143), channel_id=1, source_target_pairs={{240,0},{0,16},{16,32},{32,48},{48,64},{64,80},{80,96},{96,112},{1... | collective-permute-start | bytes 98312 | tf_op jit(solution)/shard_map/ppermute | solution.py:17
  11.4 35.5 %collective-permute-start.1 = (bf16[64,2,128]{2,0,1:T(8,128)(2,1)S(1)}, bf16[64,2,128]{2,0,1:T(8,128)(2,1)S(1)}, u32[]{:S(2)}, u32[]{:S(2)}) collective-permute-start(bf16[64,2,128]{2,0,1:T(8,128)(2,1)S(1)} %copy.143), channel_id=1, source_target_pairs={{16,0},{32,16},{48,32},{64,48},{80,64},{96,80},{112,96},{128,112},... | collective-permute-start | bytes 98312 | tf_op jit(solution)/shard_map/ppermute | solution.py:17
  11.4 150.0 %copy-start.18 = (pred[128]{0:T(512)(128)(4,1)}, pred[128]{0:T(512)(128)(4,1)S(1)}, u32[]{:S(2)}) copy-start(pred[128]{0:T(512)(128)(4,1)S(1)} %and_and_fusion.5) | copy-start | bytes 388
  11.5 150.1 %copy-start.21 = (pred[128]{0:T(512)(128)(4,1)}, pred[128]{0:T(512)(128)(4,1)S(1)}, u32[]{:S(2)}) copy-start(pred[128]{0:T(512)(128)(4,1)S(1)} %and_and_fusion.3) | copy-start | bytes 388
  11.5 150.2 %copy-start.24 = (pred[128]{0:T(512)(128)(4,1)}, pred[128]{0:T(512)(128)(4,1)S(1)}, u32[]{:S(2)}) copy-start(pred[128]{0:T(512)(128)(4,1)S(1)} %and_and_fusion.2) | copy-start | bytes 388
  12.5 34.2 %copy-start.56 = (f32[4,3,64]{2,0,1:T(4,128)S(1)}, f32[4,3,64]{2,0,1:T(4,128)}, u32[]{:S(2)}) copy-start(f32[4,3,64]{2,0,1:T(4,128)} %param.5) | copy-start | bytes 9220
  46.8 29.9 %copy-start.63 = (f32[64]{0:T(128)}, f32[64]{0:T(128)S(1)}, u32[]{:S(2)}) copy-start(f32[64]{0:T(128)S(1)} %get-tuple-element.156) | copy-start | bytes 772
  46.8 75.5 %copy-start.69 = (f32[64]{0:T(128)}, f32[64]{0:T(128)S(1)}, u32[]{:S(2)}) copy-start(f32[64]{0:T(128)S(1)} %get-tuple-element.153) | copy-start | bytes 772
  46.8 75.5 %copy-start.71 = (f32[64]{0:T(128)}, f32[64]{0:T(128)S(1)}, u32[]{:S(2)}) copy-start(f32[64]{0:T(128)S(1)} %get-tuple-element.154) | copy-start | bytes 772
  46.8 75.5 %copy-start.73 = (f32[64]{0:T(128)}, f32[64]{0:T(128)S(1)}, u32[]{:S(2)}) copy-start(f32[64]{0:T(128)S(1)} %get-tuple-element.155) | copy-start | bytes 772
  46.8 123.4 %copy-start.75 = (f32[64]{0:T(128)}, f32[64]{0:T(128)S(1)}, u32[]{:S(2)}) copy-start(f32[64]{0:T(128)S(1)} %get-tuple-element.152) | copy-start | bytes 772
  46.8 123.4 %copy-start.77 = (f32[64]{0:T(128)}, f32[64]{0:T(128)S(1)}, u32[]{:S(2)}) copy-start(f32[64]{0:T(128)S(1)} %get-tuple-element.162) | copy-start | bytes 772
  46.8 123.4 %copy-start.79 = (f32[64]{0:T(128)}, f32[64]{0:T(128)S(1)}, u32[]{:S(2)}) copy-start(f32[64]{0:T(128)S(1)} %get-tuple-element.163) | copy-start | bytes 772
  46.9 115.0 %copy-start.27 = (pred[128]{0:T(512)(128)(4,1)}, pred[128]{0:T(512)(128)(4,1)S(1)}, u32[]{:S(2)}) copy-start(pred[128]{0:T(512)(128)(4,1)S(1)} %and_and_fusion.1) | copy-start | bytes 388
  47.5 5.5 collective-permute-start.3
  48.8 113.1 %copy-start.30 = (pred[128]{0:T(512)(128)(4,1)}, pred[128]{0:T(512)(128)(4,1)S(1)}, u32[]{:S(2)}) copy-start(pred[128]{0:T(512)(128)(4,1)S(1)} %and_and_fusion) | copy-start | bytes 388
  49.0 6.0 collective-permute-start.2
  56.6 14.1 %collective-permute-start.4 = (bf16[64,2,128]{2,0,1:T(8,128)(2,1)S(1)}, bf16[64,2,128]{2,0,1:T(8,128)(2,1)S(1)}, u32[]{:S(2)}, u32[]{:S(2)}) collective-permute-start(bf16[64,2,128]{2,0,1:T(8,128)(2,1)S(1)} %fusion.164), channel_id=1, source_target_pairs={{240,0},{0,16},{16,32},{32,48},{48,64},{64,80},{80,96},{96,112},{1... | collective-permute-start | bytes 98312 | tf_op jit(solution)/shard_map/ppermute | solution.py:17
  69.7 7.0 %collective-permute-start.5 = (bf16[64,2,128]{2,0,1:T(8,128)(2,1)S(1)}, bf16[64,2,128]{2,0,1:T(8,128)(2,1)S(1)}, u32[]{:S(2)}, u32[]{:S(2)}) collective-permute-start(bf16[64,2,128]{2,0,1:T(8,128)(2,1)S(1)} %fusion.164), channel_id=1, source_target_pairs={{16,0},{32,16},{48,32},{64,48},{80,64},{96,80},{112,96},{128,112},... | collective-permute-start | bytes 98312 | tf_op jit(solution)/shard_map/ppermute | solution.py:17
  77.2 36.1 %collective-permute-start.6 = (bf16[64,2,1,128]{3,0,1,2:T(8,128)(2,1)S(1)}, bf16[64,2,1,128]{3,0,1,2:T(8,128)(2,1)S(1)}, u32[]{:S(2)}, u32[]{:S(2)}) collective-permute-start(bf16[64,2,1,128]{3,0,1,2:T(8,128)(2,1)S(1)} %bitcast.1583), channel_id=1, source_target_pairs={{0,1},{1,2},{2,3},{3,4},{4,5},{5,6},{6,7},{7,8},{8,9},{9,10},{10,1... | collective-permute-start | bytes 98312 | tf_op jit(solution)/shard_map/ppermute | solution.py:28
  80.1 33.2 %collective-permute-start.7 = (bf16[64,2,1,128]{3,0,1,2:T(8,128)(2,1)S(1)}, bf16[64,2,1,128]{3,0,1,2:T(8,128)(2,1)S(1)}, u32[]{:S(2)}, u32[]{:S(2)}) collective-permute-start(bf16[64,2,1,128]{3,0,1,2:T(8,128)(2,1)S(1)} %bitcast.1584), channel_id=1, source_target_pairs={{1,0},{2,1},{3,2},{4,3},{5,4},{6,5},{7,6},{8,7},{9,8},{10,9},{11,1... | collective-permute-start | bytes 98312 | tf_op jit(solution)/shard_map/ppermute | solution.py:30
  115.8 2.8 collective-permute-start.8
  115.8 6.5 collective-permute-start.9
  122.9 38.1 %collective-permute-start.10 = (bf16[64,2,1,128]{3,0,1,2:T(8,128)(2,1)S(1)}, bf16[64,2,1,128]{3,0,1,2:T(8,128)(2,1)S(1)}, u32[]{:S(2)}, u32[]{:S(2)}) collective-permute-start(bf16[64,2,1,128]{3,0,1,2:T(8,128)(2,1)S(1)} %bitcast.1593), channel_id=1, source_target_pairs={{0,1},{1,2},{2,3},{3,4},{4,5},{5,6},{6,7},{7,8},{8,9},{9,10},{10,1... | collective-permute-start | bytes 98312 | tf_op jit(solution)/shard_map/ppermute | solution.py:28
  125.7 35.3 %collective-permute-start.11 = (bf16[64,2,1,128]{3,0,1,2:T(8,128)(2,1)S(1)}, bf16[64,2,1,128]{3,0,1,2:T(8,128)(2,1)S(1)}, u32[]{:S(2)}, u32[]{:S(2)}) collective-permute-start(bf16[64,2,1,128]{3,0,1,2:T(8,128)(2,1)S(1)} %bitcast.1594), channel_id=1, source_target_pairs={{1,0},{2,1},{3,2},{4,3},{5,4},{6,5},{7,6},{8,7},{9,8},{10,9},{11,1... | collective-permute-start | bytes 98312 | tf_op jit(solution)/shard_map/ppermute | solution.py:30
  163.4 4.3 collective-permute-start.12
  163.5 6.8 %collective-permute-start.13 = (bf16[64,2,128]{2,0,1:T(8,128)(2,1)S(1)}, bf16[64,2,128]{2,0,1:T(8,128)(2,1)S(1)}, u32[]{:S(2)}, u32[]{:S(2)}) collective-permute-start(bf16[64,2,128]{2,0,1:T(8,128)(2,1)S(1)} %fusion.168), channel_id=1, source_target_pairs={{64,0},{80,16},{96,32},{112,48},{128,64},{144,80},{160,96},{176,11... | collective-permute-start | bytes 98312 | tf_op jit(solution)/shard_map/ppermute | solution.py:17
  170.8 36.5 %collective-permute-start.14 = (bf16[64,2,1,128]{3,0,1,2:T(8,128)(2,1)S(1)}, bf16[64,2,1,128]{3,0,1,2:T(8,128)(2,1)S(1)}, u32[]{:S(2)}, u32[]{:S(2)}) collective-permute-start(bf16[64,2,1,128]{3,0,1,2:T(8,128)(2,1)S(1)} %bitcast.1573), channel_id=1, source_target_pairs={{0,1},{1,2},{2,3},{3,4},{4,5},{5,6},{6,7},{7,8},{8,9},{9,10},{10,1... | collective-permute-start | bytes 98312 | tf_op jit(solution)/shard_map/ppermute | solution.py:28
  173.1 34.3 %collective-permute-start.15 = (bf16[64,2,1,128]{3,0,1,2:T(8,128)(2,1)S(1)}, bf16[64,2,1,128]{3,0,1,2:T(8,128)(2,1)S(1)}, u32[]{:S(2)}, u32[]{:S(2)}) collective-permute-start(bf16[64,2,1,128]{3,0,1,2:T(8,128)(2,1)S(1)} %bitcast.1574), channel_id=1, source_target_pairs={{1,0},{2,1},{3,2},{4,3},{5,4},{6,5},{7,6},{8,7},{9,8},{10,9},{11,1... | collective-permute-start | bytes 98312 | tf_op jit(solution)/shard_map/ppermute | solution.py:30
  212.9 8.3 %collective-permute-start.16 = (bf16[64,2,2,1,128]{4,0,2,1,3:T(8,128)(2,1)S(1)}, bf16[64,2,2,1,128]{4,0,2,1,3:T(8,128)(2,1)S(1)}, u32[]{:S(2)}, u32[]{:S(2)}) collective-permute-start(bf16[64,2,2,1,128]{4,0,2,1,3:T(8,128)(2,1)S(1)} %pad_maximum_fusion.40), channel_id=1, source_target_pairs={{1,0},{2,1},{3,2},{4,3},{5,4},{6,5},{7,6},{8,7},{9,8},{10,9},{11,1... | collective-permute-start | bytes 196616 | tf_op jit(solution)/shard_map/ppermute | solution.py:30
  214.5 8.4 %collective-permute-start.17 = (bf16[64,2,2,1,128]{4,0,2,1,3:T(8,128)(2,1)S(1)}, bf16[64,2,2,1,128]{4,0,2,1,3:T(8,128)(2,1)S(1)}, u32[]{:S(2)}, u32[]{:S(2)}) collective-permute-start(bf16[64,2,2,1,128]{4,0,2,1,3:T(8,128)(2,1)S(1)} %pad_maximum_fusion.40), channel_id=1, source_target_pairs={{0,1},{1,2},{2,3},{3,4},{4,5},{5,6},{6,7},{7,8},{8,9},{9,10},{10,1... | collective-permute-start | bytes 196616 | tf_op jit(solution)/shard_map/ppermute | solution.py:28
  224.5 4.3 collective-permute-start.19
  225.3 6.7 %collective-permute-start.18 = (bf16[64,2,128]{2,0,1:T(8,128)(2,1)S(1)}, bf16[64,2,128]{2,0,1:T(8,128)(2,1)S(1)}, u32[]{:S(2)}, u32[]{:S(2)}) collective-permute-start(bf16[64,2,128]{2,0,1:T(8,128)(2,1)S(1)} %get-tuple-element.48), channel_id=1, source_target_pairs={{64,0},{80,16},{96,32},{112,48},{128,64},{144,80},{160,96},{176,11... | collective-permute-start | bytes 98312 | tf_op jit(solution)/shard_map/ppermute | solution.py:17
  232.1 9.5 %collective-permute-start.20 = (bf16[64,2,2,1,128]{4,0,2,1,3:T(8,128)(2,1)S(1)}, bf16[64,2,2,1,128]{4,0,2,1,3:T(8,128)(2,1)S(1)}, u32[]{:S(2)}, u32[]{:S(2)}) collective-permute-start(bf16[64,2,2,1,128]{4,0,2,1,3:T(8,128)(2,1)S(1)} %get-tuple-element.110), channel_id=1, source_target_pairs={{1,0},{2,1},{3,2},{4,3},{5,4},{6,5},{7,6},{8,7},{9,8},{10,9},{11,1... | collective-permute-start | bytes 196616 | tf_op jit(solution)/shard_map/ppermute | solution.py:30
  236.0 5.3 collective-permute-start.21
  245.0 2.8 collective-permute-start.23
  245.6 6.4 collective-permute-start.22
  252.2 9.0 %collective-permute-start.24 = (bf16[64,2,2,1,128]{4,0,2,1,3:T(8,128)(2,1)S(1)}, bf16[64,2,2,1,128]{4,0,2,1,3:T(8,128)(2,1)S(1)}, u32[]{:S(2)}, u32[]{:S(2)}) collective-permute-start(bf16[64,2,2,1,128]{4,0,2,1,3:T(8,128)(2,1)S(1)} %pad_maximum_fusion.42), channel_id=1, source_target_pairs={{1,0},{2,1},{3,2},{4,3},{5,4},{6,5},{7,6},{8,7},{9,8},{10,9},{11,1... | collective-permute-start | bytes 196616 | tf_op jit(solution)/shard_map/ppermute | solution.py:30
  253.8 8.9 %collective-permute-start.25 = (bf16[64,2,2,1,128]{4,0,2,1,3:T(8,128)(2,1)S(1)}, bf16[64,2,2,1,128]{4,0,2,1,3:T(8,128)(2,1)S(1)}, u32[]{:S(2)}, u32[]{:S(2)}) collective-permute-start(bf16[64,2,2,1,128]{4,0,2,1,3:T(8,128)(2,1)S(1)} %pad_maximum_fusion.42), channel_id=1, source_target_pairs={{0,1},{1,2},{2,3},{3,4},{4,5},{5,6},{6,7},{7,8},{8,9},{9,10},{10,1... | collective-permute-start | bytes 196616 | tf_op jit(solution)/shard_map/ppermute | solution.py:28
  264.3 27.8 %collective-permute-start.27 = (bf16[64,2,128]{2,0,1:T(8,128)(2,1)S(1)}, bf16[64,2,128]{2,0,1:T(8,128)(2,1)S(1)}, u32[]{:S(2)}, u32[]{:S(2)}) collective-permute-start(bf16[64,2,128]{2,0,1:T(8,128)(2,1)S(1)} %get-tuple-element.46), channel_id=1, source_target_pairs={{240,0},{0,16},{16,32},{32,48},{48,64},{64,80},{80,96},{96,112},{1... | collective-permute-start | bytes 98312 | tf_op jit(solution)/shard_map/ppermute | solution.py:17
  291.1 7.0 %collective-permute-start.26 = (bf16[64,2,128]{2,0,1:T(8,128)(2,1)S(1)}, bf16[64,2,128]{2,0,1:T(8,128)(2,1)S(1)}, u32[]{:S(2)}, u32[]{:S(2)}) collective-permute-start(bf16[64,2,128]{2,0,1:T(8,128)(2,1)S(1)} %get-tuple-element.46), channel_id=1, source_target_pairs={{16,0},{32,16},{48,32},{64,48},{80,64},{96,80},{112,96},{128,112},... | collective-permute-start | bytes 98312 | tf_op jit(solution)/shard_map/ppermute | solution.py:17
  298.2 10.1 %collective-permute-start.28 = (bf16[64,2,2,1,128]{4,0,2,1,3:T(8,128)(2,1)S(1)}, bf16[64,2,2,1,128]{4,0,2,1,3:T(8,128)(2,1)S(1)}, u32[]{:S(2)}, u32[]{:S(2)}) collective-permute-start(bf16[64,2,2,1,128]{4,0,2,1,3:T(8,128)(2,1)S(1)} %pad_maximum_fusion.43), channel_id=1, source_target_pairs={{1,0},{2,1},{3,2},{4,3},{5,4},{6,5},{7,6},{8,7},{9,8},{10,9},{11,1... | collective-permute-start | bytes 196616 | tf_op jit(solution)/shard_map/ppermute | solution.py:30
  299.9 10.6 %collective-permute-start.29 = (bf16[64,2,2,1,128]{4,0,2,1,3:T(8,128)(2,1)S(1)}, bf16[64,2,2,1,128]{4,0,2,1,3:T(8,128)(2,1)S(1)}, u32[]{:S(2)}, u32[]{:S(2)}) collective-permute-start(bf16[64,2,2,1,128]{4,0,2,1,3:T(8,128)(2,1)S(1)} %pad_maximum_fusion.43), channel_id=1, source_target_pairs={{0,1},{1,2},{2,3},{3,4},{4,5},{5,6},{6,7},{7,8},{8,9},{9,10},{10,1... | collective-permute-start | bytes 196616 | tf_op jit(solution)/shard_map/ppermute | solution.py:28
  308.3 331.8 %all-reduce.35.cloned.1.call-start = ((), (), s32[]{:S(2)}) async-start(), calls=%async_computation.1 | async-start | bytes 442368 | tf_op jit(solution)/shard_map/psum | solution.py:171
  312.1 185.7 %collective-permute-start.31 = (bf16[64,2,128]{2,0,1:T(8,128)(2,1)S(1)}, bf16[64,2,128]{2,0,1:T(8,128)(2,1)S(1)}, u32[]{:S(2)}, u32[]{:S(2)}) collective-permute-start(bf16[64,2,128]{2,0,1:T(8,128)(2,1)S(1)} %get-tuple-element.45), channel_id=1, source_target_pairs={{240,0},{0,16},{16,32},{32,48},{48,64},{64,80},{80,96},{96,112},{1... | collective-permute-start | bytes 98312 | tf_op jit(solution)/shard_map/ppermute | solution.py:17
  313.1 184.7 %collective-permute-start.30 = (bf16[64,2,128]{2,0,1:T(8,128)(2,1)S(1)}, bf16[64,2,128]{2,0,1:T(8,128)(2,1)S(1)}, u32[]{:S(2)}, u32[]{:S(2)}) collective-permute-start(bf16[64,2,128]{2,0,1:T(8,128)(2,1)S(1)} %get-tuple-element.45), channel_id=1, source_target_pairs={{16,0},{32,16},{48,32},{64,48},{80,64},{96,80},{112,96},{128,112},... | collective-permute-start | bytes 98312 | tf_op jit(solution)/shard_map/ppermute | solution.py:17
  (67 other events, 176.4 us)
Sparse Core Ops, SparseCore 0:
  308.4 183.0 all-reduce.32
  497.9 142.1 all-reduce.34
where the time goes:
time: 651 us; the launch traced here: 649 us
  waiting for transfers between devices  264 us (41%)
  blocking collectives  216 us (33%)
  starting transfers between devices  93.6 us (14%)
  local copies, waits for them, and re-layouts  28.6 us (4%)
  between operations  16.5 us (3%)
  other arithmetic  15.3 us (2%)
  matrix products  14.9 us (2%)
    psum x1, waiting for transfers between devices, per_device(): grad_kernel = lax.psum(kernel_piece, 'phase').astype(jnp.float32)  141 us
    all_gather x4, blocking collectives, per_device(): kernel = lax.all_gather(conv_weights[block_num], 'chan', axis=3, tiled=True)  130 us
    unnamed x3, waiting for transfers between devices  91.4 us
    psum x1, blocking collectives, per_device(): grad_taps = lax.psum(jnp.stack(tap_grads), ('phase', 'chan'))  85.8 us
    ppermute x16, starting transfers between devices, shifted(): return lax.ppermute(block, axis, route)  53.4 us
    ppermute x16, waiting for transfers between devices, shifted(): return lax.ppermute(block, axis, route)  31.2 us
    ppermute x8, starting transfers between devices, padded_2(): lax.ppermute(tail, axis, [(i, (i + 1) % count) for i in range(ends)])  29.5 us
    unnamed x172, local copies, waits for them, and re-layouts  20.6 us
  transfers between devices with their start and end apart: 34, of which 15 were waited for; matrix products, arithmetic and copies ran while one was open for 4% of the time, Pallas kernels for 0%

commit v1 on v0

--- a/solution.py
+++ b/solution.py
@@ -172,7 +172,9 @@
         weight_grads[block_num] = grad_kernel
         tap_grads[block_num] = grad_tap
     grad_weights = jnp.stack(weight_grads)
-    grad_taps = lax.psum(jnp.stack(tap_grads), ("phase", "chan"))
+    x = jnp.stack(tap_grads)
+    parts = lax.all_gather(x, ("phase", "chan"))
+    grad_taps = jnp.sum(parts, axis=0)
     return (state, grad_state, grad_taps, grad_weights)
 
 

time: 651 us -> 1090 us (1.67)
  blocking collectives: 216 us -> 655 us
  waiting for transfers between devices: 264 us -> 279 us
  local copies, waits for them, and re-layouts: 28.6 us -> 15.7 us
    all_gather x0 -> x1, blocking collectives: none -> 523 us  [per_device(): parts = lax.all_gather(x, ('phase', 'chan'))]
    psum x1, waiting for transfers between devices: 141 us -> 247 us  [per_device(): grad_kernel = lax.psum(kernel_piece, 'phase').astype(jnp.float32)]
    unnamed x3, waiting for transfers between devices: 91.4 us -> 0.03 us
    psum x1 -> x0, blocking collectives: 85.8 us -> none  [per_device(): grad_taps = lax.psum(jnp.stack(tap_grads), ('phase', 'chan'))]
    unnamed x172 -> x170, local copies, waits for them, and re-layouts: 20.6 us -> 6.78 us
  transfers between devices with their start and end apart: 34 -> 34, of which waited for: 15 -> 14; matrix products, arithmetic and copies ran while one was open for 4% -> 3% of each run, Pallas kernels for 0% -> 0%
where the time goes in v1:
time: 1090 us
  blocking collectives  655 us (60%)
  waiting for transfers between devices  279 us (26%)
  starting transfers between devices  92.3 us (8%)
  other arithmetic  19.1 us (2%)
  between operations  16.8 us (2%)
  local copies, waits for them, and re-layouts  15.7 us (1%)
  matrix products  14.8 us (1%)
    all_gather x1, blocking collectives, per_device(): parts = lax.all_gather(x, ('phase', 'chan'))  523 us
    psum x1, waiting for transfers between devices, per_device(): grad_kernel = lax.psum(kernel_piece, 'phase').astype(jnp.float32)  247 us
    all_gather x4, blocking collectives, per_device(): kernel = lax.all_gather(conv_weights[block_num], 'chan', axis=3, tiled=True)  131 us
    ppermute x16, starting transfers between devices, shifted(): return lax.ppermute(block, axis, route)  54.2 us
    ppermute x16, waiting for transfers between devices, shifted(): return lax.ppermute(block, axis, route)  31.7 us
    ppermute x8, starting transfers between devices, padded_2(): lax.ppermute(tail, axis, [(i, (i + 1) % count) for i in range(ends)])  27.7 us
  transfers between devices with their start and end apart: 34, of which 14 were waited for; matrix products, arithmetic and copies ran while one was open for 3% of the time, Pallas kernels for 0%

profile of v1, /device:TPU:7, one launch (start us, length us, event | category | flops | bytes accessed | tf_op | source)
XLA Modules:
  0.0 1092.8 jit_solution(2123093030799779049)
XLA Ops:
  8.0 3.4 collective-permute-start
  12.5 34.2 %all-gather = bf16[1,64,27,2,64]{1,3,2,0,4:T(2,128)(2,1)S(1)} all-gather(bf16[1,64,27,2,4]{1,3,2,0,4:T(2,128)(2,1)S(1)} %copy.557), channel_id=2, replica_groups=mesh['phase'=16,'chan'=16] {'chan'}, dimensions={4}, use_global_device_ids=true | all-gather | bytes 470016 | tf_op jit(solution)/shard_map/all_gather | solution.py:109
  48.2 1.3 collective-permute-start.3
  49.7 4.0 collective-permute-start.2
  56.4 13.0 %collective-permute-start.4 = (bf16[64,2,128]{2,0,1:T(8,128)(2,1)S(1)}, bf16[64,2,128]{2,0,1:T(8,128)(2,1)S(1)}, u32[]{:S(2)}, u32[]{:S(2)}) collective-permute-start(bf16[64,2,128]{2,0,1:T(8,128)(2,1)S(1)} %fusion.164), channel_id=1, source_target_pairs={{240,0},{0,16},{16,32},{32,48},{48,64},{64,80},{80,96},{96,112},{1... | collective-permute-start | bytes 98312 | tf_op jit(solution)/shard_map/ppermute | solution.py:17
  70.5 5.9 collective-permute-done.5
  76.5 3.3 collective-permute-start.6
  79.8 1.3 collective-permute-start.7
  81.1 31.8 %all-gather.1 = bf16[1,64,27,2,64]{1,3,2,0,4:T(2,128)(2,1)S(1)} all-gather(bf16[1,64,27,2,4]{1,3,2,0,4:T(2,128)(2,1)S(1)} %copy.558), channel_id=3, replica_groups=mesh['phase'=16,'chan'=16] {'chan'}, dimensions={4}, use_global_device_ids=true | all-gather | bytes 470016 | tf_op jit(solution)/shard_map/all_gather | solution.py:109
  115.1 1.5 collective-permute-start.9
  116.6 1.3 collective-permute-done.8
  117.9 3.7 collective-permute-done.9
  122.2 2.6 collective-permute-start.10
  124.8 1.3 collective-permute-start.11
  126.2 32.6 %all-gather.2 = bf16[1,64,27,2,64]{1,3,2,0,4:T(2,128)(2,1)S(1)} all-gather(bf16[1,64,27,2,4]{1,3,2,0,4:T(2,128)(2,1)S(1)} %copy.559), channel_id=4, replica_groups=mesh['phase'=16,'chan'=16] {'chan'}, dimensions={4}, use_global_device_ids=true | all-gather | bytes 470016 | tf_op jit(solution)/shard_map/all_gather | solution.py:109
  161.0 3.0 collective-permute-start.13
  164.0 1.3 collective-permute-done.12
  165.3 2.6 collective-permute-done.13
  168.0 1.3 collective-permute-start.14
  169.3 1.3 collective-permute-start.15
  170.6 32.9 %all-gather.3 = bf16[1,64,27,2,64]{1,3,2,0,4:T(2,128)(2,1)S(1)} all-gather(bf16[1,64,27,2,4]{1,3,2,0,4:T(2,128)(2,1)S(1)} %copy.560), channel_id=5, replica_groups=mesh['phase'=16,'chan'=16] {'chan'}, dimensions={4}, use_global_device_ids=true | all-gather | bytes 470016 | tf_op jit(solution)/shard_map/all_gather | solution.py:109
  203.8 1.3 dynamic-slice
  210.9 1.3 collective-permute-start.16
  212.5 4.0 collective-permute-start.17
  218.0 1.1 pad_maximum_fusion.3
  222.5 2.6 collective-permute-start.18
  226.4 2.7 collective-permute-done.18
  229.3 1.3 collective-permute-start.20
  231.8 4.0 collective-permute-start.21
  235.8 1.1 pad_maximum_fusion.2
  239.8 1.2 collective-permute-start.23
  242.6 4.8 collective-permute-done.22
  247.6 1.3 collective-permute-start.24
  249.1 4.0 collective-permute-start.25
  254.0 1.1 pad_maximum_fusion.1
  257.8 27.6 %collective-permute-start.27 = (bf16[64,2,128]{2,0,1:T(8,128)(2,1)S(1)}, bf16[64,2,128]{2,0,1:T(8,128)(2,1)S(1)}, u32[]{:S(2)}, u32[]{:S(2)}) collective-permute-start(bf16[64,2,128]{2,0,1:T(8,128)(2,1)S(1)} %get-tuple-element.46), channel_id=1, source_target_pairs={{240,0},{0,16},{16,32},{32,48},{48,64},{64,80},{80,96},{96,112},{1... | collective-permute-start | bytes 98312 | tf_op jit(solution)/shard_map/ppermute | solution.py:17
  285.4 1.0 collective-permute-done.27
  286.4 5.9 collective-permute-done.26
  292.5 1.3 collective-permute-start.28
  294.1 4.6 collective-permute-start.29
  299.6 1.2 pad_maximum_fusion
  305.1 523.3 %all-gather.4 = f32[1024,3,64]{2,1,0:T(4,128)S(1)} all-gather(f32[4,3,64]{2,1,0:T(4,128)S(1)} %pad_maximum_fusion.48), channel_id=6, replica_groups=mesh['phase'=16,'chan'=16] {'phase','chan'}, dimensions={0}, use_global_device_ids=true | all-gather | bytes 789504 | tf_op jit(solution)/shard_map/all_gather | solution.py:176
  829.5 1.5 dynamic-slice_bitcast_fusion
  831.1 1.6 dynamic-slice_bitcast_fusion.1
  832.6 1.5 dynamic-slice_bitcast_fusion.2
  834.2 1.6 dynamic-slice_bitcast_fusion.3
  836.6 247.4 %all-reduce.35.cloned.1.call-done = (bf16[1,64,27,2,4]{1,4,2,3,0:T(4,128)(2,1)}, bf16[1,64,27,2,4]{1,4,2,3,0:T(4,128)(2,1)}, bf16[1,64,27,2,4]{1,4,2,3,0:T(4,128)(2,1)}, bf16[1,64,27,2,4]{1,4,2,3,0:T(4,128)(2,1)}) async-done(((bf16[1,64,27,2,4]{1,4,2,3,0:T(4,128)(2,1)}, bf16[1,64,27,2,4]{1,4,2,3,0:T(4,128)(2,1)}, bf16[1,64,27,2,4]{1,4,2,3,0:T(4,128)(2,1)}, bf16[1,64,27,2,4]{1,4,2,3,0:T(4,128)(2,1)}), ...) | async-done | bytes 110608 | tf_op jit(solution)/shard_map/psum | solution.py:171
  1084.0 1.1 maximum_convert_fusion
  (372 shorter events, 41.2 us)
Async XLA Ops:
  7.2 822.4 %all-reduce.33.cloned.1.call-start = ((), (), s32[]{:S(2)}) async-start(), calls=%async_computation | async-start | bytes 7077888
  8.0 39.8 %collective-permute-start = (bf16[64,2,128]{2,0,1:T(8,128)(2,1)S(1)}, bf16[64,2,128]{2,0,1:T(8,128)(2,1)S(1)}, u32[]{:S(2)}, u32[]{:S(2)}) collective-permute-start(bf16[64,2,128]{2,0,1:T(8,128)(2,1)S(1)} %copy.142), channel_id=1, source_target_pairs={{240,0},{0,16},{16,32},{32,48},{48,64},{64,80},{80,96},{96,112},{1... | collective-permute-start | bytes 98312 | tf_op jit(solution)/shard_map/ppermute | solution.py:17
  11.4 36.4 %collective-permute-start.1 = (bf16[64,2,128]{2,0,1:T(8,128)(2,1)S(1)}, bf16[64,2,128]{2,0,1:T(8,128)(2,1)S(1)}, u32[]{:S(2)}, u32[]{:S(2)}) collective-permute-start(bf16[64,2,128]{2,0,1:T(8,128)(2,1)S(1)} %copy.142), channel_id=1, source_target_pairs={{16,0},{32,16},{48,32},{64,48},{80,64},{96,80},{112,96},{128,112},... | collective-permute-start | bytes 98312 | tf_op jit(solution)/shard_map/ppermute | solution.py:17
  11.4 147.9 %copy-start.18 = (pred[128]{0:T(512)(128)(4,1)}, pred[128]{0:T(512)(128)(4,1)S(1)}, u32[]{:S(2)}) copy-start(pred[128]{0:T(512)(128)(4,1)S(1)} %and_and_fusion.5) | copy-start | bytes 388
  11.5 148.1 %copy-start.21 = (pred[128]{0:T(512)(128)(4,1)}, pred[128]{0:T(512)(128)(4,1)S(1)}, u32[]{:S(2)}) copy-start(pred[128]{0:T(512)(128)(4,1)S(1)} %and_and_fusion.3) | copy-start | bytes 388
  11.5 148.2 %copy-start.24 = (pred[128]{0:T(512)(128)(4,1)}, pred[128]{0:T(512)(128)(4,1)S(1)}, u32[]{:S(2)}) copy-start(pred[128]{0:T(512)(128)(4,1)S(1)} %and_and_fusion.2) | copy-start | bytes 388
  47.6 74.0 %copy-start.68 = (f32[64]{0:T(128)}, f32[64]{0:T(128)S(1)}, u32[]{:S(2)}) copy-start(f32[64]{0:T(128)S(1)} %get-tuple-element.153) | copy-start | bytes 772
  47.7 74.0 %copy-start.70 = (f32[64]{0:T(128)}, f32[64]{0:T(128)S(1)}, u32[]{:S(2)}) copy-start(f32[64]{0:T(128)S(1)} %get-tuple-element.154) | copy-start | bytes 772
  47.7 73.9 %copy-start.72 = (f32[64]{0:T(128)}, f32[64]{0:T(128)S(1)}, u32[]{:S(2)}) copy-start(f32[64]{0:T(128)S(1)} %get-tuple-element.155) | copy-start | bytes 772
  47.7 120.2 %copy-start.74 = (f32[64]{0:T(128)}, f32[64]{0:T(128)S(1)}, u32[]{:S(2)}) copy-start(f32[64]{0:T(128)S(1)} %get-tuple-element.152) | copy-start | bytes 772
  47.7 120.2 %copy-start.76 = (f32[64]{0:T(128)}, f32[64]{0:T(128)S(1)}, u32[]{:S(2)}) copy-start(f32[64]{0:T(128)S(1)} %get-tuple-element.162) | copy-start | bytes 772
  47.7 120.2 %copy-start.78 = (f32[64]{0:T(128)}, f32[64]{0:T(128)S(1)}, u32[]{:S(2)}) copy-start(f32[64]{0:T(128)S(1)} %get-tuple-element.163) | copy-start | bytes 772
  47.7 112.1 %copy-start.27 = (pred[128]{0:T(512)(128)(4,1)}, pred[128]{0:T(512)(128)(4,1)S(1)}, u32[]{:S(2)}) copy-start(pred[128]{0:T(512)(128)(4,1)S(1)} %and_and_fusion.1) | copy-start | bytes 388
  48.2 5.5 collective-permute-start.3
  49.5 110.4 %copy-start.30 = (pred[128]{0:T(512)(128)(4,1)}, pred[128]{0:T(512)(128)(4,1)S(1)}, u32[]{:S(2)}) copy-start(pred[128]{0:T(512)(128)(4,1)S(1)} %and_and_fusion) | copy-start | bytes 388
  49.7 5.6 collective-permute-start.2
  56.4 14.1 %collective-permute-start.4 = (bf16[64,2,128]{2,0,1:T(8,128)(2,1)S(1)}, bf16[64,2,128]{2,0,1:T(8,128)(2,1)S(1)}, u32[]{:S(2)}, u32[]{:S(2)}) collective-permute-start(bf16[64,2,128]{2,0,1:T(8,128)(2,1)S(1)} %fusion.164), channel_id=1, source_target_pairs={{240,0},{0,16},{16,32},{32,48},{48,64},{64,80},{80,96},{96,112},{1... | collective-permute-start | bytes 98312 | tf_op jit(solution)/shard_map/ppermute | solution.py:17
  69.5 7.0 collective-permute-start.5
  76.5 36.6 %collective-permute-start.6 = (bf16[64,2,1,128]{3,0,1,2:T(8,128)(2,1)S(1)}, bf16[64,2,1,128]{3,0,1,2:T(8,128)(2,1)S(1)}, u32[]{:S(2)}, u32[]{:S(2)}) collective-permute-start(bf16[64,2,1,128]{3,0,1,2:T(8,128)(2,1)S(1)} %bitcast.1585), channel_id=1, source_target_pairs={{0,1},{1,2},{2,3},{3,4},{4,5},{5,6},{6,7},{7,8},{8,9},{9,10},{10,1... | collective-permute-start | bytes 98312 | tf_op jit(solution)/shard_map/ppermute | solution.py:28
  79.8 33.3 %collective-permute-start.7 = (bf16[64,2,1,128]{3,0,1,2:T(8,128)(2,1)S(1)}, bf16[64,2,1,128]{3,0,1,2:T(8,128)(2,1)S(1)}, u32[]{:S(2)}, u32[]{:S(2)}) collective-permute-start(bf16[64,2,1,128]{3,0,1,2:T(8,128)(2,1)S(1)} %bitcast.1586), channel_id=1, source_target_pairs={{1,0},{2,1},{3,2},{4,3},{5,4},{6,5},{7,6},{8,7},{9,8},{10,9},{11,1... | collective-permute-start | bytes 98312 | tf_op jit(solution)/shard_map/ppermute | solution.py:30
  115.1 2.8 collective-permute-start.8
  115.1 6.5 collective-permute-start.9
  122.2 36.8 %collective-permute-start.10 = (bf16[64,2,1,128]{3,0,1,2:T(8,128)(2,1)S(1)}, bf16[64,2,1,128]{3,0,1,2:T(8,128)(2,1)S(1)}, u32[]{:S(2)}, u32[]{:S(2)}) collective-permute-start(bf16[64,2,1,128]{3,0,1,2:T(8,128)(2,1)S(1)} %bitcast.1595), channel_id=1, source_target_pairs={{0,1},{1,2},{2,3},{3,4},{4,5},{5,6},{6,7},{7,8},{8,9},{9,10},{10,1... | collective-permute-start | bytes 98312 | tf_op jit(solution)/shard_map/ppermute | solution.py:28
  124.8 34.1 %collective-permute-start.11 = (bf16[64,2,1,128]{3,0,1,2:T(8,128)(2,1)S(1)}, bf16[64,2,1,128]{3,0,1,2:T(8,128)(2,1)S(1)}, u32[]{:S(2)}, u32[]{:S(2)}) collective-permute-start(bf16[64,2,1,128]{3,0,1,2:T(8,128)(2,1)S(1)} %bitcast.1596), channel_id=1, source_target_pairs={{1,0},{2,1},{3,2},{4,3},{5,4},{6,5},{7,6},{8,7},{9,8},{10,9},{11,1... | collective-permute-start | bytes 98312 | tf_op jit(solution)/shard_map/ppermute | solution.py:30
  160.9 4.3 collective-permute-start.12
  161.0 6.9 collective-permute-start.13
  168.0 37.7 %collective-permute-start.14 = (bf16[64,2,1,128]{3,0,1,2:T(8,128)(2,1)S(1)}, bf16[64,2,1,128]{3,0,1,2:T(8,128)(2,1)S(1)}, u32[]{:S(2)}, u32[]{:S(2)}) collective-permute-start(bf16[64,2,1,128]{3,0,1,2:T(8,128)(2,1)S(1)} %bitcast.1575), channel_id=1, source_target_pairs={{0,1},{1,2},{2,3},{3,4},{4,5},{5,6},{6,7},{7,8},{8,9},{9,10},{10,1... | collective-permute-start | bytes 98312 | tf_op jit(solution)/shard_map/ppermute | solution.py:28
  169.3 36.4 %collective-permute-start.15 = (bf16[64,2,1,128]{3,0,1,2:T(8,128)(2,1)S(1)}, bf16[64,2,1,128]{3,0,1,2:T(8,128)(2,1)S(1)}, u32[]{:S(2)}, u32[]{:S(2)}) collective-permute-start(bf16[64,2,1,128]{3,0,1,2:T(8,128)(2,1)S(1)} %bitcast.1576), channel_id=1, source_target_pairs={{1,0},{2,1},{3,2},{4,3},{5,4},{6,5},{7,6},{8,7},{9,8},{10,9},{11,1... | collective-permute-start | bytes 98312 | tf_op jit(solution)/shard_map/ppermute | solution.py:30
  210.9 8.3 collective-permute-start.16
  212.5 8.4 collective-permute-start.17
  222.0 4.4 collective-permute-start.19
  222.5 6.7 collective-permute-start.18
  229.3 8.0 collective-permute-start.20
  231.8 5.3 collective-permute-start.21
  239.8 2.8 collective-permute-start.23
  241.0 6.4 collective-permute-start.22
  247.6 7.6 collective-permute-start.24
  249.1 7.6 collective-permute-start.25
  257.8 28.6 %collective-permute-start.27 = (bf16[64,2,128]{2,0,1:T(8,128)(2,1)S(1)}, bf16[64,2,128]{2,0,1:T(8,128)(2,1)S(1)}, u32[]{:S(2)}, u32[]{:S(2)}) collective-permute-start(bf16[64,2,128]{2,0,1:T(8,128)(2,1)S(1)} %get-tuple-element.46), channel_id=1, source_target_pairs={{240,0},{0,16},{16,32},{32,48},{48,64},{64,80},{80,96},{96,112},{1... | collective-permute-start | bytes 98312 | tf_op jit(solution)/shard_map/ppermute | solution.py:17
  285.4 7.0 collective-permute-start.26
  292.5 8.3 collective-permute-start.28
  294.1 9.0 collective-permute-start.29
  300.8 783.2 %all-reduce.35.cloned.1.call-start = ((), (), s32[]{:S(2)}) async-start(), calls=%async_computation.1 | async-start | bytes 442368 | tf_op jit(solution)/shard_map/psum | solution.py:171
  304.1 531.7 %collective-permute-start.31 = (bf16[64,2,128]{2,0,1:T(8,128)(2,1)S(1)}, bf16[64,2,128]{2,0,1:T(8,128)(2,1)S(1)}, u32[]{:S(2)}, u32[]{:S(2)}) collective-permute-start(bf16[64,2,128]{2,0,1:T(8,128)(2,1)S(1)} %get-tuple-element.45), channel_id=1, source_target_pairs={{240,0},{0,16},{16,32},{32,48},{48,64},{64,80},{80,96},{96,112},{1... | collective-permute-start | bytes 98312 | tf_op jit(solution)/shard_map/ppermute | solution.py:17
  305.1 530.7 %collective-permute-start.30 = (bf16[64,2,128]{2,0,1:T(8,128)(2,1)S(1)}, bf16[64,2,128]{2,0,1:T(8,128)(2,1)S(1)}, u32[]{:S(2)}, u32[]{:S(2)}) collective-permute-start(bf16[64,2,128]{2,0,1:T(8,128)(2,1)S(1)} %get-tuple-element.45), channel_id=1, source_target_pairs={{16,0},{32,16},{48,32},{64,48},{80,64},{96,80},{112,96},{128,112},... | collective-permute-start | bytes 98312 | tf_op jit(solution)/shard_map/ppermute | solution.py:17
  305.1 530.7 %copy-start.57 = (f32[64]{0:T(128)S(1)}, f32[64]{0:T(128)}, u32[]{:S(2)}) copy-start(f32[64]{0:T(128)} %copy-done.56) | copy-start | bytes 772
  305.1 530.7 %copy-start.59 = (f32[64]{0:T(128)S(1)}, f32[64]{0:T(128)}, u32[]{:S(2)}) copy-start(f32[64]{0:T(128)} %copy-done.58) | copy-start | bytes 772
  305.1 530.7 %copy-start.61 = (f32[64]{0:T(128)S(1)}, f32[64]{0:T(128)}, u32[]{:S(2)}) copy-start(f32[64]{0:T(128)} %copy-done.60) | copy-start | bytes 772
  (66 other events, 916.9 us)
Sparse Core Ops, SparseCore 0:
  300.9 195.4 all-reduce.32
  835.9 248.0 all-reduce.34
